TPU v7x, 32 devices: a whole 2x2x4 slice. The times are simulated.
32 devices in a mesh: queue: 8 (over z, y), mp: 4 (over x, core).
Axes of the slice: x: 2, y: 2, z: 4, core: 2. Of those that a mesh axis runs over, the one named last changes fastest.
Arguments:
- state: bfloat16 [8, 512, 3072], P('queue', None, 'mp')
- key_cache: bfloat16 [8, 32, 3072], P('queue', None, 'mp'), as said below
- value_cache: bfloat16 [8, 32, 3072], P('queue', None, 'mp'), may hold values from -15 to 15
- level_gain: float32 [50, 3072], P(None, 'mp'), may hold values from 0.25 to 1.75
- sigma: float32 [51], replicated, may hold values from 0.05 to 1.5
- levels: int32 [8], P('queue'), may hold values from 0 to 49
- group_len: int32 [8], replicated, may hold values from 256 to 512, as said below
- ctx_ids: int32 [8, 6], P('queue'), may hold values from 0 to 6, as said below
- ctx_count: int32 [8], P('queue'), may hold values from 0 to 6, as said below
Outputs:
- advanced: bfloat16 [8, 512, 3072], P('queue', None, 'mp')
Inputs may be any that keep to these rules, and one draw needn't show every extreme that they name: `group_len`: some group has exactly 512 live tokens. `ctx_count`: slot c lists at most min(c, 6) blocks, and the last slot lists exactly 6. `ctx_ids`: the first ctx_count[c] entries of slot c are distinct blocks of index below c; the other entries are 0. `key_cache`: keys of the clean context blocks.
All inputs are finite; a program needn't handle non-finite values.
Results may differ from a plain program's by a relative error of at most 0.015.
The roundings to bfloat16 on the way count: a program that leaves them out, or rounds other values in their place, can miss the bound.
Values may be sent and summed in bfloat16 or wider, within the bound.
No kernel may reach another device: no remote copies, remote signals or barrier semaphores. Data moves between devices by JAX's collectives and lax.ppermute only.
A program may use at most 64 MiB of HBM per device.

v0:
```python
import jax
import jax.numpy as jnp
from jax import lax
from jax.sharding import PartitionSpec as P

HEAD_DIM = 128
FEAT = 3072
STEPS = 2


def shifted(array, axis, by):
    peers = lax.axis_size(axis)
    return lax.ppermute(array, axis, [(i, (i + by) % peers) for i in range(peers)])


def absorb(state_carry, queries, all_keys, all_values, key_live):
    running_max, running_sum, weighted = state_carry
    heads_here = running_max.shape[0]
    scaling = HEAD_DIM ** (-0.5)

    def one_head(inputs):
        head_index, max_head, sum_head, weighted_head = inputs
        query_head = lax.dynamic_slice_in_dim(queries, head_index * HEAD_DIM, HEAD_DIM, 1)
        key_head = lax.dynamic_slice_in_dim(all_keys, head_index * HEAD_DIM, HEAD_DIM, 1)
        value_head = lax.dynamic_slice_in_dim(all_values, head_index * HEAD_DIM, HEAD_DIM, 1)
        scores = (
            jnp.einsum("rd,kd->rk", query_head, key_head, preferred_element_type=jnp.float32)
            * scaling
        )
        scores = jnp.where(key_live[None, :], scores, -jnp.inf)
        new_max = jnp.maximum(max_head, jnp.max(scores, axis=1))
        weights = jnp.exp(scores - new_max[:, None])
        factor = jnp.exp(max_head - new_max)
        new_sum = sum_head * factor + jnp.sum(weights, axis=1)
        new_weighted = weighted_head * factor[:, None] + jnp.dot(
            weights.astype(jnp.bfloat16), value_head, preferred_element_type=jnp.float32
        )
        return (new_max, new_sum, new_weighted)

    return lax.map(one_head, (jnp.arange(heads_here), running_max, running_sum, weighted))


def on_device(
    state, key_cache, value_cache, level_gain, sigma, levels, group_len, ctx_ids, ctx_count
):
    row_count = state.shape[1]
    feature_count = state.shape[2]
    block_rows = key_cache.shape[1]
    heads_here = feature_count // HEAD_DIM
    groups = lax.axis_size("queue")
    slot_index = lax.axis_index("queue")
    block_index = jnp.arange(groups)
    sigma_index = jnp.arange(sigma.shape[0])
    level_range = jnp.arange(level_gain.shape[0])
    level_now, ids_now, count_now = (levels, ctx_ids, ctx_count)
    current = state[0]
    for step_index in range(STEPS):
        if step_index > 0:
            level_now, ids_now, count_now = shifted((level_now, ids_now, count_now), "queue", -1)
        level_index = level_now[0]
        level_pick = (level_range == level_index).astype(jnp.float32)
        gain_row = jnp.dot(level_pick[None, :], level_gain, precision=lax.Precision.HIGHEST)
        step_size = jnp.sum(jnp.where(sigma_index == level_index + 1, sigma, 0.0)) - jnp.sum(
            jnp.where(sigma_index == level_index, sigma, 0.0)
        )
        block_list = ids_now[0]
        list_live = jnp.arange(block_list.shape[0]) < count_now[0]
        length = jnp.sum(jnp.where(block_index == slot_index, group_len, 0))
        token_live = jnp.arange(row_count) < length
        widened = current.astype(jnp.float32)
        squares = lax.psum(jnp.sum(widened * widened, axis=1), "mp")
        normed = widened * lax.rsqrt(squares / FEAT + 1e-06)[:, None]
        queries = (normed * gain_row).astype(jnp.bfloat16)
        own_keys = normed.astype(jnp.bfloat16)
        empty_carry = (
            jnp.full((heads_here, row_count), -jnp.inf, jnp.float32),
            jnp.zeros((heads_here, row_count), jnp.float32),
            jnp.zeros((heads_here, row_count, HEAD_DIM), jnp.float32),
        )
        state_carry = absorb(empty_carry, queries, own_keys, current, token_live)
        listed = jnp.any((block_list[:, None] == block_index[None, :]) & list_live[:, None], axis=0)
        key_piece = lax.all_gather(key_cache, "queue", axis=0, tiled=True)
        value_piece = lax.all_gather(value_cache, "queue", axis=0, tiled=True)
        block_count = key_piece.shape[0]
        piece_live = jnp.repeat(listed, block_rows)
        state_carry = absorb(
            state_carry,
            queries,
            key_piece.reshape(block_count * block_rows, feature_count),
            value_piece.reshape(block_count * block_rows, feature_count),
            piece_live,
        )
        running_max, running_sum, weighted = state_carry
        attended = jnp.transpose(weighted / running_sum[:, :, None], (1, 0, 2)).reshape(
            row_count, feature_count
        )
        advanced_rows = jnp.where(token_live[:, None], widened + step_size * attended, widened)
        updated = advanced_rows.astype(jnp.bfloat16)
        current = updated
    current = shifted(current, "queue", STEPS)
    return current[None]


def solution(mesh):
    in_specs = (
        P("queue", None, "mp"),
        P("queue", None, "mp"),
        P("queue", None, "mp"),
        P(None, "mp"),
        P(),
        P("queue"),
        P(),
        P("queue", None),
        P("queue"),
    )
    out_specs = P("queue", None, "mp")
    return jax.shard_map(
        on_device, mesh=mesh, in_specs=in_specs, out_specs=out_specs, check_vma=False
    )
```

profile of v0, /device:TPU:0, one launch (start us, length us, event | category | flops | bytes accessed | tf_op | source)
XLA Modules:
  0.0 237.5 jit_solution(6927961134695069647)
XLA Ops:
  0.0 6.0 %collective-permute-start.1 = (s32[1,6]{1,0:T(1,128)}, s32[1,6]{1,0:T(1,128)S(1)}, u32[]{:S(2)}, u32[]{:S(2)}) collective-permute-start(s32[1,6]{1,0:T(1,128)} %param.24), channel_id=1, source_target_pairs={{0,28},{4,0},{8,4},{12,8},{16,12},{20,16},{24,20},{28,24},{1,29},{... | collective-permute-start | bytes 80 | tf_op jit(solution)/shard_map/ppermute | solution.py:13
  6.5 1.4 collective-permute-start.2
  11.2 33.4 %all_gather.8 = bf16[8,32,768]{2,1,0:T(8,128)(2,1)} all-gather(bf16[1,32,768]{2,1,0:T(8,128)(2,1)} %param.18), channel_id=1, replica_groups=mesh['queue'=8,'mp'=4] {'queue'}, dimensions={0}, use_global_device_ids=true | all-gather | bytes 442368 | tf_op jit(solution)/shard_map/all_gather | solution.py:82
  44.6 31.3 %all_gather.9 = bf16[8,32,768]{2,1,0:T(8,128)(2,1)S(1)} all-gather(bf16[1,32,768]{2,1,0:T(8,128)(2,1)} %param.19), channel_id=1, replica_groups=mesh['queue'=8,'mp'=4] {'queue'}, dimensions={0}, use_global_device_ids=true | all-gather | bytes 442368 | tf_op jit(solution)/shard_map/all_gather | solution.py:83
  75.9 1.4 copy.36
  77.5 5.7 %psum.14 = f32[512]{0:T(512)S(1)} all-reduce(f32[512]{0:T(512)S(1)} %fusion.66), channel_id=1, replica_groups=mesh['queue'=8,'mp'=4] {'mp'}, use_global_device_ids=true, to_apply=%region_4.5 | all-reduce | flops 512 | bytes 4096 | tf_op jit(solution)/shard_map/psum | solution.py:71
  86.0 33.6 %while.56 = (s32[]{:T(128)}, f32[6,512]{1,0:T(8,128)S(1)}, f32[6,512]{1,0:T(8,128)S(1)}, f32[6,512,128]{2,1,0:T(8,128)}, s32[6]{0:T(128)S(1)}, /*index=5*/bf16[5...) while((s32[]{:T(128)}, f32[6,512]{1,0:T(8,128)S(1)}, ...), condition=%wide.region_8.9_spmd.clone, body=%wide.region_5.8_spmd.clone.sunk | while | flops 136120320 | bytes 3832019 | solution.py:40
  89.7 1.9 fusion.120
  95.2 2.0 fusion.120
  100.8 2.0 fusion.120
  106.4 2.0 fusion.120
  112.0 2.0 fusion.120
  117.6 2.0 fusion.120
  119.9 24.9 %while.57 = (s32[]{:T(128)}, f32[6,512]{1,0:T(8,128)S(1)}, f32[6,512,128]{1,2,0:T(8,128)S(1)}, f32[6,512]{1,0:T(8,128)S(1)}, f32[6,512]{1,0:T(8,128)S(1)}, /*ind...) while((s32[]{:T(128)}, f32[6,512]{1,0:T(8,128)S(1)}, ...), condition=%wide.region_13.14_spmd.clone, body=%wide.region_10.13_spmd.clone.sunk | while | flops 68159488 | bytes 3447023 | solution.py:40
  150.1 6.6 %psum.15 = f32[512]{0:T(512)S(1)} all-reduce(f32[512]{0:T(512)S(1)} %get-tuple-element.529), channel_id=1, replica_groups=mesh['queue'=8,'mp'=4] {'mp'}, use_global_device_ids=true, to_apply=%region_17.18 | all-reduce | flops 512 | bytes 4096 | tf_op jit(solution)/shard_map/psum | solution.py:71
  160.2 28.3 %while.58 = (s32[]{:T(128)}, f32[6,512]{1,0:T(8,128)S(1)}, f32[6,512]{1,0:T(8,128)S(1)}, f32[6,512,128]{2,1,0:T(8,128)}, s32[6]{0:T(128)S(1)}, /*index=5*/bf16[5...) while((s32[]{:T(128)}, f32[6,512]{1,0:T(8,128)S(1)}, ...), condition=%wide.region_21.22_spmd.clone, body=%wide.region_18.21_spmd.clone.sunk | while | flops 136120320 | bytes 3832019 | solution.py:40
  162.2 1.3 fusion.129
  166.9 1.3 fusion.129
  171.6 1.3 fusion.129
  176.3 1.3 fusion.129
  181.0 1.3 fusion.129
  185.7 1.3 fusion.129
  189.9 25.6 %while.59 = (s32[]{:T(128)}, f32[6,512]{1,0:T(8,128)S(1)}, f32[6,512,128]{1,2,0:T(8,128)S(1)}, f32[6,512]{1,0:T(8,128)S(1)}, f32[6,512]{1,0:T(8,128)S(1)}, /*ind...) while((s32[]{:T(128)}, f32[6,512]{1,0:T(8,128)S(1)}, ...), condition=%wide.region_26.27_spmd.clone, body=%wide.region_23.26_spmd.clone.sunk | while | flops 68159488 | bytes 3447023 | solution.py:40
  216.1 20.2 %collective-permute-done.3 = bf16[512,768]{0,1:T(8,128)(2,1)S(1)} collective-permute-done((bf16[512,768]{0,1:T(8,128)(2,1)S(1)}, bf16[512,768]{0,1:T(8,128)(2,1)S(1)}, u32[]{:S(2)}, u32[]{:S(2)}) %collective-permute-start.3) | collective-permute-done | bytes 786464 | tf_op jit(solution)/shard_map/ppermute | solution.py:13
  (288 shorter events, 90.3 us)
Async XLA Ops:
  0.0 83.2 %copy-start = (f32[50,768]{1,0:T(8,128)S(1)}, f32[50,768]{1,0:T(8,128)}, u32[]{:S(2)}) copy-start(f32[50,768]{1,0:T(8,128)} %param.20) | copy-start | bytes 460804
  0.0 189.6 %collective-permute-start.1 = (s32[1,6]{1,0:T(1,128)}, s32[1,6]{1,0:T(1,128)S(1)}, u32[]{:S(2)}, u32[]{:S(2)}) collective-permute-start(s32[1,6]{1,0:T(1,128)} %param.24), channel_id=1, source_target_pairs={{0,28},{4,0},{8,4},{12,8},{16,12},{20,16},{24,20},{28,24},{1,29},{... | collective-permute-start | bytes 80 | tf_op jit(solution)/shard_map/ppermute | solution.py:13
  6.0 138.8 %collective-permute-start = (s32[1]{0:T(128)}, s32[1]{0:T(128)}, u32[]{:S(2)}, u32[]{:S(2)}) collective-permute-start(s32[1]{0:T(128)} %param.22), channel_id=1, source_target_pairs={{0,28},{4,0},{8,4},{12,8},{16,12},{20,16},{24,20},{28,24},{1,29},{... | collective-permute-start | bytes 20 | tf_op jit(solution)/shard_map/ppermute | solution.py:13
  6.5 139.7 %collective-permute-start.2 = (s32[1]{0:T(128)}, s32[1]{0:T(128)}, u32[]{:S(2)}, u32[]{:S(2)}) collective-permute-start(s32[1]{0:T(128)} %param.25), channel_id=1, source_target_pairs={{0,28},{4,0},{8,4},{12,8},{16,12},{20,16},{24,20},{28,24},{1,29},{... | collective-permute-start | bytes 20 | tf_op jit(solution)/shard_map/ppermute | solution.py:13
  86.0 33.6 %copy-start.3 = (s32[1,6]{1,0:T(1,128)S(1)}, s32[1,6]{1,0:T(1,128)}, u32[]{:S(2)}) copy-start(s32[1,6]{1,0:T(1,128)} %param.24) | copy-start | bytes 76
  119.9 27.0 %copy-start.2 = (f32[51]{0:T(128)S(1)}, f32[51]{0:T(128)}, u32[]{:S(2)}) copy-start(f32[51]{0:T(128)} %param.21) | copy-start | bytes 616
  144.8 4.8 %copy-start.1 = (bf16[256,768]{1,0:T(8,128)(2,1)}, bf16[256,768]{1,0:T(8,128)(2,1)S(1)}, u32[]{:S(2)}) copy-start(bf16[256,768]{1,0:T(8,128)(2,1)S(1)} %get-tuple-element.980) | copy-start | bytes 1179652
  216.0 20.3 %collective-permute-start.3 = (bf16[512,768]{0,1:T(8,128)(2,1)S(1)}, bf16[512,768]{0,1:T(8,128)(2,1)S(1)}, u32[]{:S(2)}, u32[]{:S(2)}) collective-permute-start(bf16[512,768]{0,1:T(8,128)(2,1)S(1)} %fusion.69), channel_id=1, source_target_pairs={{0,8},{4,12},{8,16},{12,20},{16,24},{20,28},{24,0},{28,4},{1,9},{5... | collective-permute-start | bytes 2359304 | tf_op jit(solution)/shard_map/ppermute | solution.py:13
where the time goes:
time: 239 us; the launch traced here: 237 us
  blocking collectives  76.9 us (32%)
  matrix products  63.6 us (27%)
  local copies, waits for them, and re-layouts  28.8 us (12%)
  waiting for transfers between devices  20.2 us (8%)
  other arithmetic  18.5 us (8%)
  loops' own time  16.9 us (7%)
  starting transfers between devices  8 us (3%)
  between operations  4.54 us (2%)
    all_gather x1, blocking collectives, on_device(): key_piece = lax.all_gather(key_cache, 'queue', axis=0, tiled=True)  33.4 us
    dot_general x24, matrix products, one_head(): jnp.dot(weights.astype(jnp.bfloat16), value_head, preferred_element_type=...  33.2 us
    all_gather x1, blocking collectives, on_device(): value_piece = lax.all_gather(value_cache, 'queue', axis=0, tiled=True)  31.3 us
    dot_general x24, matrix products, one_head(): jnp.einsum('rd,kd->rk', query_head, key_head, preferred_element_type=jnp....  29.5 us
    ppermute x4, waiting for transfers between devices, shifted(): lax.ppermute(array, axis, [(i, (i + by) % peers) for i in range(peers)])  20.2 us
    another operation x4, loops' own time, absorb(): lax.map(one_head, (jnp.arange(heads_here), running_max, running_sum, weig...  16.9 us
    dynamic_slice x36, local copies, waits for them, and re-layouts, absorb(): lax.map(one_head, (jnp.arange(heads_here), running_max, running_sum, weig...  15 us
    psum x2, blocking collectives, on_device(): squares = lax.psum(jnp.sum(widened * widened, axis=1), 'mp')  12.3 us
  transfers between devices with their start and end apart: 4, of which 1 were waited for; matrix products, arithmetic and copies ran while one was open for 37% of the time, Pallas kernels for 0%

commit v1 on v0

--- a/solution.py
+++ b/solution.py
@@ -6,6 +6,29 @@
 HEAD_DIM = 128
 FEAT = 3072
 STEPS = 2
+
+
+def in_order(blocks, dim):
+    blocks = jnp.moveaxis(blocks, 0, dim)
+    shape = blocks.shape
+    return blocks.reshape(*shape[:dim], shape[dim] * shape[dim + 1], *shape[dim + 2 :])
+
+
+def doubled(value, axis):
+    peers, position = (lax.axis_size(axis), lax.axis_index(axis))
+    tiles, stride = (value[None], 1)
+    while stride < peers:
+        partner_block = lax.ppermute(tiles, axis, [(i, i ^ stride) for i in range(peers)])
+        low = position & stride == 0
+        tiles = jnp.concatenate(
+            [jnp.where(low, tiles, partner_block), jnp.where(low, partner_block, tiles)]
+        )
+        stride *= 2
+    return tiles
+
+
+def collect(x, axis, dim):
+    return in_order(doubled(x, axis), dim)
 
 
 def shifted(array, axis, by):
@@ -79,7 +102,7 @@
         )
         state_carry = absorb(empty_carry, queries, own_keys, current, token_live)
         listed = jnp.any((block_list[:, None] == block_index[None, :]) & list_live[:, None], axis=0)
-        key_piece = lax.all_gather(key_cache, "queue", axis=0, tiled=True)
+        key_piece = collect(key_cache, "queue", 0)
         value_piece = lax.all_gather(value_cache, "queue", axis=0, tiled=True)
         block_count = key_piece.shape[0]
         piece_live = jnp.repeat(listed, block_rows)

time: 239 us -> 219 us (0.916)
  blocking collectives: 76.9 us -> 43.6 us
  waiting for transfers between devices: 20.2 us -> 33.8 us
    all_gather x1 -> x0, blocking collectives: 33.4 us -> none  [on_device(): key_piece = lax.all_gather(key_cache, 'queue', axis=0, tiled=True)]
    ppermute x0 -> x3, waiting for transfers between devices: none -> 13.6 us  [doubled(): lax.ppermute(tiles, axis, [(i, i ^ stride) for i in range(peers)])]
  transfers between devices with their start and end apart: 4 -> 7, of which waited for: 1 -> 3; matrix products, arithmetic and copies ran while one was open for 37% -> 17% of each run, Pallas kernels for 0% -> 0%
where the time goes in v1:
time: 219 us; the launch traced here: 218 us
  matrix products  63.6 us (29%)
  blocking collectives  43.6 us (20%)
  waiting for transfers between devices  33.8 us (15%)
  local copies, waits for them, and re-layouts  28.5 us (13%)
  other arithmetic  19.4 us (9%)
  loops' own time  15.6 us (7%)
  starting transfers between devices  8.77 us (4%)
  between operations  4.46 us (2%)
    dot_general x24, matrix products, one_head(): jnp.dot(weights.astype(jnp.bfloat16), value_head, preferred_element_type=...  33.2 us
    all_gather x1, blocking collectives, on_device(): value_piece = lax.all_gather(value_cache, 'queue', axis=0, tiled=True)  31.4 us
    dot_general x24, matrix products, one_head(): jnp.einsum('rd,kd->rk', query_head, key_head, preferred_element_type=jnp....  29.5 us
    ppermute x4, waiting for transfers between devices, shifted(): lax.ppermute(array, axis, [(i, (i + by) % peers) for i in range(peers)])  20.2 us
    another operation x4, loops' own time, absorb(): lax.map(one_head, (jnp.arange(heads_here), running_max, running_sum, weig...  15.6 us
    dynamic_slice x36, local copies, waits for them, and re-layouts, absorb(): lax.map(one_head, (jnp.arange(heads_here), running_max, running_sum, weig...  14.1 us
    ppermute x3, waiting for transfers between devices, doubled(): lax.ppermute(tiles, axis, [(i, i ^ stride) for i in range(peers)])  13.6 us
    psum x2, blocking collectives, on_device(): squares = lax.psum(jnp.sum(widened * widened, axis=1), 'mp')  12.2 us
  transfers between devices with their start and end apart: 7, of which 3 were waited for; matrix products, arithmetic and copies ran while one was open for 17% of the time, Pallas kernels for 0%

profile of v1, /device:TPU:0, one launch (start us, length us, event | category | flops | bytes accessed | tf_op | source)
XLA Modules:
  0.0 217.7 jit_solution(9713797245042593530)
XLA Ops:
  0.0 6.0 %collective-permute-start.4 = (s32[1,6]{1,0:T(1,128)}, s32[1,6]{1,0:T(1,128)S(1)}, u32[]{:S(2)}, u32[]{:S(2)}) collective-permute-start(s32[1,6]{1,0:T(1,128)} %param.24), channel_id=1, source_target_pairs={{0,28},{4,0},{8,4},{12,8},{16,12},{20,16},{24,20},{28,24},{1,29},{... | collective-permute-start | bytes 80 | tf_op jit(solution)/shard_map/ppermute | solution.py:36
  6.5 1.4 collective-permute-start.5
  11.8 31.4 %all_gather.4 = bf16[8,32,768]{2,1,0:T(8,128)(2,1)S(1)} all-gather(bf16[1,32,768]{2,1,0:T(8,128)(2,1)} %param.19), channel_id=1, replica_groups=mesh['queue'=8,'mp'=4] {'queue'}, dimensions={0}, use_global_device_ids=true | all-gather | bytes 442368 | tf_op jit(solution)/shard_map/all_gather | solution.py:106
  43.2 1.4 copy.36
  44.8 5.7 %psum.14 = f32[512]{0:T(512)S(1)} all-reduce(f32[512]{0:T(512)S(1)} %fusion.66), channel_id=1, replica_groups=mesh['queue'=8,'mp'=4] {'mp'}, use_global_device_ids=true, to_apply=%region_4.5 | all-reduce | flops 512 | bytes 4096 | tf_op jit(solution)/shard_map/psum | solution.py:94
  53.3 32.3 %while.56 = (s32[]{:T(128)}, f32[6,512]{1,0:T(8,128)S(1)}, f32[6,512]{1,0:T(8,128)S(1)}, f32[6,512,128]{2,1,0:T(8,128)}, s32[6]{0:T(128)S(1)}, /*index=5*/bf16[5...) while((s32[]{:T(128)}, f32[6,512]{1,0:T(8,128)S(1)}, ...), condition=%wide.region_8.9_spmd.clone, body=%wide.region_5.8_spmd.clone.sunk | while | flops 136120320 | bytes 3832019 | solution.py:63
  56.8 1.9 fusion.120
  62.1 2.0 fusion.120
  67.5 2.0 fusion.120
  72.9 2.0 fusion.120
  78.3 2.0 fusion.120
  83.7 2.0 fusion.120
  90.8 3.8 %collective-permute-done.1 = bf16[2,1,32,768]{3,2,1,0:T(8,128)(2,1)S(1)} collective-permute-done((bf16[2,1,32,768]{3,2,1,0:T(8,128)(2,1)S(1)}, bf16[2,1,32,768]{3,2,1,0:T(8,128)(2,1)S(1)}, u32[]{:S(2)}, u32[]{:S(2)}) %collective-permute-start.1) | collective-permute-done | bytes 98336 | tf_op jit(solution)/shard_map/ppermute | solution.py:21
  95.6 9.8 %collective-permute-done.2 = bf16[4,1,32,768]{3,2,1,0:T(8,128)(2,1)S(1)} collective-permute-done((bf16[4,1,32,768]{3,2,1,0:T(8,128)(2,1)S(1)}, bf16[4,1,32,768]{3,2,1,0:T(8,128)(2,1)S(1)}, u32[]{:S(2)}, u32[]{:S(2)}) %collective-permute-start.2) | collective-permute-done | bytes 196640 | tf_op jit(solution)/shard_map/ppermute | solution.py:21
  106.4 24.9 %while.57 = (s32[]{:T(128)}, f32[6,512]{1,0:T(8,128)S(1)}, f32[6,512,128]{1,2,0:T(8,128)S(1)}, f32[6,512]{1,0:T(8,128)S(1)}, f32[6,512]{1,0:T(8,128)S(1)}, /*ind...) while((s32[]{:T(128)}, f32[6,512]{1,0:T(8,128)S(1)}, ...), condition=%wide.region_13.14_spmd.clone, body=%wide.region_10.13_spmd.clone.sunk | while | flops 68159488 | bytes 3447023 | solution.py:63
  132.5 6.6 %psum.15 = f32[512]{0:T(512)S(1)} all-reduce(f32[512]{0:T(512)S(1)} %get-tuple-element.529), channel_id=1, replica_groups=mesh['queue'=8,'mp'=4] {'mp'}, use_global_device_ids=true, to_apply=%region_17.18 | all-reduce | flops 512 | bytes 4096 | tf_op jit(solution)/shard_map/psum | solution.py:94
  142.6 27.4 %while.58 = (s32[]{:T(128)}, f32[6,512]{1,0:T(8,128)S(1)}, f32[6,512]{1,0:T(8,128)S(1)}, f32[6,512,128]{2,1,0:T(8,128)}, s32[6]{0:T(128)S(1)}, /*index=5*/bf16[5...) while((s32[]{:T(128)}, f32[6,512]{1,0:T(8,128)S(1)}, ...), condition=%wide.region_21.22_spmd.clone, body=%wide.region_18.21_spmd.clone.sunk | while | flops 136120320 | bytes 3832019 | solution.py:63
  144.4 1.3 fusion.129
  149.0 1.3 fusion.129
  153.5 1.3 fusion.129
  162.6 1.3 fusion.129
  167.2 1.3 fusion.129
  170.2 25.6 %while.59 = (s32[]{:T(128)}, f32[6,512]{1,0:T(8,128)S(1)}, f32[6,512,128]{1,2,0:T(8,128)S(1)}, f32[6,512]{1,0:T(8,128)S(1)}, f32[6,512]{1,0:T(8,128)S(1)}, /*ind...) while((s32[]{:T(128)}, f32[6,512]{1,0:T(8,128)S(1)}, ...), condition=%wide.region_26.27_spmd.clone, body=%wide.region_23.26_spmd.clone.sunk | while | flops 68159488 | bytes 3447023 | solution.py:63
  196.4 20.2 %collective-permute-done.6 = bf16[512,768]{0,1:T(8,128)(2,1)S(1)} collective-permute-done((bf16[512,768]{0,1:T(8,128)(2,1)S(1)}, bf16[512,768]{0,1:T(8,128)(2,1)S(1)}, u32[]{:S(2)}, u32[]{:S(2)}) %collective-permute-start.6) | collective-permute-done | bytes 786464 | tf_op jit(solution)/shard_map/ppermute | solution.py:36
  (301 shorter events, 92.9 us)
Async XLA Ops:
  0.0 50.5 %copy-start = (f32[50,768]{1,0:T(8,128)S(1)}, f32[50,768]{1,0:T(8,128)}, u32[]{:S(2)}) copy-start(f32[50,768]{1,0:T(8,128)} %param.20) | copy-start | bytes 460804
  0.0 95.5 %collective-permute-start.4 = (s32[1,6]{1,0:T(1,128)}, s32[1,6]{1,0:T(1,128)S(1)}, u32[]{:S(2)}, u32[]{:S(2)}) collective-permute-start(s32[1,6]{1,0:T(1,128)} %param.24), channel_id=1, source_target_pairs={{0,28},{4,0},{8,4},{12,8},{16,12},{20,16},{24,20},{28,24},{1,29},{... | collective-permute-start | bytes 80 | tf_op jit(solution)/shard_map/ppermute | solution.py:36
  6.0 79.7 %collective-permute-start.3 = (s32[1]{0:T(128)}, s32[1]{0:T(128)}, u32[]{:S(2)}, u32[]{:S(2)}) collective-permute-start(s32[1]{0:T(128)} %param.22), channel_id=1, source_target_pairs={{0,28},{4,0},{8,4},{12,8},{16,12},{20,16},{24,20},{28,24},{1,29},{... | collective-permute-start | bytes 20 | tf_op jit(solution)/shard_map/ppermute | solution.py:36
  6.5 88.3 %collective-permute-start.5 = (s32[1]{0:T(128)}, s32[1]{0:T(128)}, u32[]{:S(2)}, u32[]{:S(2)}) collective-permute-start(s32[1]{0:T(128)} %param.25), channel_id=1, source_target_pairs={{0,28},{4,0},{8,4},{12,8},{16,12},{20,16},{24,20},{28,24},{1,29},{... | collective-permute-start | bytes 20 | tf_op jit(solution)/shard_map/ppermute | solution.py:36
  7.9 82.0 %collective-permute-start = (bf16[1,1,32,768]{3,2,1,0:T(8,128)(2,1)}, bf16[1,1,32,768]{3,2,1,0:T(8,128)(2,1)S(1)}, u32[]{:S(2)}, u32[]{:S(2)}) collective-permute-start(bf16[1,1,32,768]{3,2,1,0:T(8,128)(2,1)} %bitcast.129), channel_id=1, source_target_pairs={{0,4},{4,0},{8,12},{12,8},{16,20},{20,16},{24,28},{28,24},{1,5},{5... | collective-permute-start | bytes 147464 | tf_op jit(solution)/shard_map/ppermute | solution.py:21
  53.3 32.3 %copy-start.4 = (s32[1,6]{1,0:T(1,128)S(1)}, s32[1,6]{1,0:T(1,128)}, u32[]{:S(2)}) copy-start(s32[1,6]{1,0:T(1,128)} %param.24) | copy-start | bytes 76
  53.3 33.0 %copy-start.3 = (f32[51]{0:T(128)S(1)}, f32[51]{0:T(128)}, u32[]{:S(2)}) copy-start(f32[51]{0:T(128)} %param.21) | copy-start | bytes 616
  53.3 36.6 %copy-start.2 = (bf16[1,32,768]{2,1,0:T(8,128)(2,1)S(1)}, bf16[1,32,768]{2,1,0:T(8,128)(2,1)}, u32[]{:S(2)}) copy-start(bf16[1,32,768]{2,1,0:T(8,128)(2,1)} %param.18) | copy-start | bytes 147460
  90.0 4.7 %collective-permute-start.1 = (bf16[2,1,32,768]{3,2,1,0:T(8,128)(2,1)S(1)}, bf16[2,1,32,768]{3,2,1,0:T(8,128)(2,1)S(1)}, u32[]{:S(2)}, u32[]{:S(2)}) collective-permute-start(bf16[2,1,32,768]{3,2,1,0:T(8,128)(2,1)S(1)} %pad_maximum_fusion.2), channel_id=1, source_target_pairs={{0,8},{4,12},{8,0},{12,4},{16,24},{20,28},{24,16},{28,20},{1,9},{5... | collective-permute-start | bytes 294920 | tf_op jit(solution)/shard_map/ppermute | solution.py:21
  94.7 10.7 %collective-permute-start.2 = (bf16[4,1,32,768]{3,2,1,0:T(8,128)(2,1)S(1)}, bf16[4,1,32,768]{3,2,1,0:T(8,128)(2,1)S(1)}, u32[]{:S(2)}, u32[]{:S(2)}) collective-permute-start(bf16[4,1,32,768]{3,2,1,0:T(8,128)(2,1)S(1)} %pad_maximum_fusion.1), channel_id=1, source_target_pairs={{0,16},{4,20},{8,24},{12,28},{16,0},{20,4},{24,8},{28,12},{1,17},{... | collective-permute-start | bytes 589832 | tf_op jit(solution)/shard_map/ppermute | solution.py:21
  131.3 0.8 copy-start.1
  196.3 20.2 %collective-permute-start.6 = (bf16[512,768]{0,1:T(8,128)(2,1)S(1)}, bf16[512,768]{0,1:T(8,128)(2,1)S(1)}, u32[]{:S(2)}, u32[]{:S(2)}) collective-permute-start(bf16[512,768]{0,1:T(8,128)(2,1)S(1)} %fusion.69), channel_id=1, source_target_pairs={{0,8},{4,12},{8,16},{12,20},{16,24},{20,28},{24,0},{28,4},{1,9},{5... | collective-permute-start | bytes 2359304 | tf_op jit(solution)/shard_map/ppermute | solution.py:36
